TPU v7x, 32 devices: a whole 2x2x4 slice. The times are simulated.
32 devices in a mesh: echo: 4 (over y, x), space: 8 (over z, core).
Axes of the slice: x: 2, y: 2, z: 4, core: 2. Of those that a mesh axis runs over, the one named last changes fastest.
Arguments:
- coil_images: bfloat16 [2, 8, 16, 64, 256, 256], P(None, None, 'echo', 'space')
- sensitivities: bfloat16 [2, 16, 64, 256, 256], P(None, 'echo', 'space'), may hold values from -0.72 to 0.72
- mask: int32 [64, 256, 256], P('space'), may hold values 0 or 1
- echo_order: int32 [8], replicated, may hold values from 0 to 7, as said below
Outputs:
- field_map: float32 [64, 256, 256], P('space')
- susceptibility: float32 [64, 256, 256], P('space')
Inputs may be any that keep to these rules, and one draw needn't show every extreme that they name: echo_order holds every echo number from 0 to 7 exactly once.
All inputs are finite; a program needn't handle non-finite values. No bound on the sum of `mask` on one device may be relied on, other than what follows from the above.
Results may differ from a plain program's by a relative error of at most 0.0003.
Values sent between devices are 32-bit elements; how exact they have to be, the bound alone decides.
A program may use at most 320 MiB of HBM per device.

v0:
```python
import math

import jax
import jax.numpy as jnp
from jax import lax
from jax.sharding import PartitionSpec as P

ITERS = 2


power_floor = 0.5
tikhonov = 0.05


def fit_field(sums_real, sums_imag, coil_power, mask_values, echo_order):
    inverse_power = 1.0 / jnp.maximum(coil_power, power_floor)
    image_real = sums_real * inverse_power[None]
    image_imag = sums_imag * inverse_power[None]
    echo_count = sums_real.shape[0]
    onehot = (echo_order[None, :] == jnp.arange(echo_count, dtype=jnp.int32)[:, None]).astype(
        jnp.float32
    )
    ordered_real = jnp.einsum("ks,szxy->kzxy", onehot, image_real, precision=lax.Precision.HIGHEST)
    ordered_imag = jnp.einsum("ks,szxy->kzxy", onehot, image_imag, precision=lax.Precision.HIGHEST)
    numerator = jnp.sum(
        ordered_real[:-1] * ordered_imag[1:] - ordered_imag[:-1] * ordered_real[1:], axis=0
    )
    echo_power = ordered_real * ordered_real + ordered_imag * ordered_imag
    denominator = 1.0 + jnp.sum(0.5 * (echo_power[:-1] + echo_power[1:]), axis=0)
    return mask_values.astype(jnp.float32) * numerator / denominator


def signed_frequency(positions, length):
    shifted = jnp.where(positions < length // 2, positions, positions - length)
    return shifted.astype(jnp.float32) / length


def kernel_values(z_index, x_index, y_index, depth_len, rows_len, cols_len):
    freq_z = signed_frequency(z_index, depth_len)[:, None, None]
    freq_x = signed_frequency(x_index, rows_len)[None, :, None]
    freq_y = signed_frequency(y_index, cols_len)[None, None, :]
    anchor = (
        (z_index[:, None, None] == 0)
        & (x_index[None, :, None] == 0)
        & (y_index[None, None, :] == 0)
    ).astype(jnp.float32)
    total = freq_z * freq_z + freq_x * freq_x + freq_y * freq_y
    return 1.0 / 3.0 - freq_z * freq_z / (total + anchor)


def transform(values, axis_pos, inverse):
    length = values.shape[axis_pos]
    pattern = ("", "zxy,zk->kxy", "zxy,xk->zky", "zxy,yk->zxk")[axis_pos]
    positions = jnp.arange(length, dtype=jnp.int32)
    product_mod = positions[:, None] * positions[None, :] % length
    radians = 2.0 * math.pi / length * product_mod.astype(jnp.float32)
    table_cos = jnp.cos(radians)
    table_sin = jnp.sin(radians)

    def contract_axis(operand, table):
        return jnp.einsum(pattern, operand, table, precision=lax.Precision.HIGHEST)

    real_in = values[0]
    imag_in = values[1]
    if inverse:
        real_out = (contract_axis(real_in, table_cos) - contract_axis(imag_in, table_sin)) / length
        imag_out = (contract_axis(imag_in, table_cos) + contract_axis(real_in, table_sin)) / length
    else:
        real_out = contract_axis(real_in, table_cos) + contract_axis(imag_in, table_sin)
        imag_out = contract_axis(imag_in, table_cos) - contract_axis(real_in, table_sin)
    return jnp.stack([real_out, imag_out])


def full_dipole_map(vector, dipole_kernel):
    complex_field = jnp.stack([vector, jnp.zeros_like(vector)])
    complex_field = transform(complex_field, 3, False)
    complex_field = transform(complex_field, 2, False)
    pencils = transform(
        lax.all_to_all(complex_field, "space", split_axis=2, concat_axis=1, tiled=True), 1, False
    )
    pencils = transform(pencils * dipole_kernel[None], 1, True)
    slabs = lax.all_to_all(pencils, "space", split_axis=1, concat_axis=2, tiled=True)
    slabs = transform(slabs, 2, True)
    slabs = transform(slabs, 3, True)
    return slabs[0]


def on_device(coil_images, sensitivities, mask, echo_order):
    sens_real = sensitivities[0]
    sens_imag = sensitivities[1]
    image_real = coil_images[0]
    image_imag = coil_images[1]

    def coil_contract(sens_part, image_part):
        return jnp.einsum(
            "czxy,eczxy->ezxy", sens_part, image_part, preferred_element_type=jnp.float32
        )

    sums_real = coil_contract(sens_real, image_real) + coil_contract(sens_imag, image_imag)
    sums_imag = coil_contract(sens_real, image_imag) - coil_contract(sens_imag, image_real)
    power_part = jnp.einsum(
        "czxy,czxy->zxy", sens_real, sens_real, preferred_element_type=jnp.float32
    )
    power_part = power_part + jnp.einsum(
        "czxy,czxy->zxy", sens_imag, sens_imag, preferred_element_type=jnp.float32
    )
    total_real, total_imag, coil_power = lax.psum((sums_real, sums_imag, power_part), "echo")
    field_map = fit_field(total_real, total_imag, coil_power, mask, echo_order)
    depth_len = field_map.shape[0] * lax.axis_size("space")
    rows_len = field_map.shape[1]
    cols_len = field_map.shape[2]
    pencil_rows = rows_len // lax.axis_size("space")
    x_index = lax.axis_index("space") * pencil_rows + jnp.arange(pencil_rows, dtype=jnp.int32)
    z_index = jnp.arange(depth_len, dtype=jnp.int32)
    weights = mask.astype(jnp.float32)
    dipole_kernel = kernel_values(
        z_index, x_index, jnp.arange(cols_len, dtype=jnp.int32), depth_len, rows_len, cols_len
    )

    def dipole_map(vector):
        return full_dipole_map(vector, dipole_kernel)

    right = dipole_map(weights * field_map)
    susceptibility = jnp.zeros_like(right)
    residual = right
    direction = right
    old_norm = lax.psum(jnp.sum(residual * residual), "space")
    for iteration in range(ITERS):
        product_image = dipole_map(weights * dipole_map(direction)) + tikhonov * direction
        curvature = lax.psum(jnp.sum(direction * product_image), "space")
        step_size = old_norm / curvature
        susceptibility = susceptibility + step_size * direction
        residual = residual - step_size * product_image
        new_norm = lax.psum(jnp.sum(residual * residual), "space")
        direction = residual + new_norm / old_norm * direction
        old_norm = new_norm
    return (field_map, susceptibility)


def solution(mesh):
    placed = (
        P(None, None, "echo", "space", None, None),
        P(None, "echo", "space", None, None),
        P("space", None, None),
        P(),
    )
    return jax.shard_map(
        on_device,
        mesh=mesh,
        in_specs=placed,
        out_specs=(P("space", None, None), P("space", None, None)),
        check_vma=False,
    )
```

profile of v0, /device:TPU:0, one launch (start us, length us, event | category | flops | bytes accessed | tf_op | source)
XLA Modules:
  0.0 2256.6 jit_solution(2206045303448730448)
XLA Ops:
  7.2 11.5 bitcast_convert_fusion.1
  18.7 6.0 multiply_reduce_fusion
  24.7 42.5 %fusion = (f32[8,256,256,8]{2,1,0,3:T(8,128)}, f32[8,256,256,8]{2,1,0,3:T(8,128)}) fusion(f32[8,256,256,4]{2,1,0,3:T(8,128)} %get-tuple-element.15, bf16[2,8,4,8,256,256]{5,4,3,2,1,0:T(8,128)(2,1)} %param.4), kind=kLoop, calls=%fused_computation.4 | loop fusion | flops 92274688 | bytes 109051904
  67.2 42.5 %fusion.2 = (f32[8,256,256,8]{2,1,0,3:T(8,128)}, f32[8,256,256,8]{2,1,0,3:T(8,128)}) fusion(f32[8,256,256,4]{2,1,0,3:T(8,128)} %get-tuple-element.16, bf16[2,8,4,8,256,256]{5,4,3,2,1,0:T(8,128)(2,1)} %param.4), kind=kLoop, calls=%fused_computation.6 | loop fusion | flops 92274688 | bytes 109051904
  112.9 87.9 %fusion.8 = (f32[8,8,256,256]{3,0,2,1:T(8,128)}, f32[8,8,256,256]{3,0,2,1:T(8,128)}) fusion(f32[8,256,256,8]{2,1,0,3:T(8,128)} %get-tuple-element.5, f32[8,256,256,8]{2,1,0,3:T(8,128)} %get-tuple-element.3, f32[8,256,256,8]{2,1,0,3:T(8,128)} %get-tuple-element.4, f32[8,256,256,8]{2,1,0,3:T(8,128)} %get-tuple-element.2), kind=kLoop, calls=%fused_computation.16 | loop fusion | flops 8388608 | bytes 100663296 | tf_op jit(solution)/shard_map/sub | solution.py:100
  200.9 4.1 fusion.123
  207.8 610.3 %all-reduce.4.cloned.1.call-done = (f32[8,8,256,256]{3,0,2,1:T(8,128)}, f32[8,256,256]{2,1,0:T(8,128)}, f32[8,8,256,256]{3,0,2,1:T(8,128)}) async-done(((f32[8,8,256,256]{3,0,2,1:T(8,128)}, f32[8,256,256]{2,1,0:T(8,128)}, f32[8,8,256,256]{3,0,2,1:T(8,128)}), (f32[8,8,256,256]{3,0,2,1:T(8,128)}, f32[8,256,256]{2,1,0:T(8,128)}, f32[8,8,256,256]{3,0,2,1:T(8,128)})) %all-reduce.4.cloned.1.call-update) | async-done | bytes 35651600 | tf_op jit(solution)/shard_map/psum | solution.py:107
  821.3 15.3 fusion.12
  836.7 27.6 %multiply_add_fusion = (f32[8,8,256,256]{3,0,2,1:T(8,128)}, f32[8,8,256,256]{3,0,2,1:T(8,128)}) fusion(f32[8,8,256,256]{3,0,2,1:T(8,128)} %fusion.12, f32[8,8,256,256]{3,0,2,1:T(8,128)} %get-tuple-element.12, f32[8,256,256]{2,1,0:T(8,128)} %maximum_divide_fusion, s32[8]{0:T(128)S(1)} %copy-done.14), kind=kOutput, calls=%fused_computation.19 | convolution fusion | flops 419430464 | bytes 69206048 | tf_op jit(solution)/shard_map/ks,szxy->kzxy/dot_general | solution.py:24
  864.2 27.6 %fusion.7 = f32[8,256,256]{2,1,0:T(8,128)S(1)} fusion(f32[8,8,256,256]{3,0,2,1:T(8,128)} %fusion.12, f32[8,8,256,256]{3,0,2,1:T(8,128)} %get-tuple-element.28), kind=kLoop, calls=%fused_computation.13 | loop fusion | flops 14155776 | bytes 60817408 | tf_op jit(solution)/shard_map/reduce_sum | solution.py:25
  891.8 16.5 fusion.5
  928.0 4.4 copy.130
  932.4 4.8 all-to-all-start
  938.1 93.0 %all-to-all-done = f32[2,8,256,256]{3,1,0,2:T(8,128)} async-done(((f32[2,8,256,256]{3,1,0,2:T(8,128)}), f32[2,8,256,256]{3,1,0,2:T(8,128)}, u32[]{:S(2)}, u32[]{:S(2)}) %all-to-all-start) | async-done | bytes 4194336 | tf_op jit(solution)/shard_map/all_to_all | solution.py:79
  1055.2 96.5 %all_to_all.150 = f32[2,64,32,256]{3,2,0,1:T(8,128)S(1)} all-to-all(f32[2,64,32,256]{3,2,0,1:T(8,128)S(1)} %copy.132), channel_id=1, replica_groups=mesh['echo'=4,'space'=8] {'space'}, dimensions={1} | all-to-all | bytes 8388608 | tf_op jit(solution)/shard_map/all_to_all | solution.py:82
  1176.5 3.3 fusion.193
  1191.7 96.5 %all_to_all.151 = f32[2,8,256,256]{3,1,0,2:T(8,128)S(1)} all-to-all(f32[2,8,256,256]{3,1,0,2:T(8,128)S(1)} %copy.144), channel_id=1, replica_groups=mesh['echo'=4,'space'=8] {'space'}, dimensions={2} | all-to-all | bytes 8388608 | tf_op jit(solution)/shard_map/all_to_all | solution.py:79
  1310.1 96.5 %all_to_all.152 = f32[2,64,32,256]{3,2,0,1:T(8,128)S(1)} all-to-all(f32[2,64,32,256]{3,2,0,1:T(8,128)S(1)} %copy.146), channel_id=1, replica_groups=mesh['echo'=4,'space'=8] {'space'}, dimensions={1} | all-to-all | bytes 8388608 | tf_op jit(solution)/shard_map/all_to_all | solution.py:82
  1431.5 3.3 fusion.197
  1446.6 96.5 %all_to_all.153 = f32[2,8,256,256]{3,1,0,2:T(8,128)S(1)} all-to-all(f32[2,8,256,256]{3,1,0,2:T(8,128)S(1)} %copy.158), channel_id=1, replica_groups=mesh['echo'=4,'space'=8] {'space'}, dimensions={2} | all-to-all | bytes 8388608 | tf_op jit(solution)/shard_map/all_to_all | solution.py:79
  1564.9 96.5 %all_to_all.154 = f32[2,64,32,256]{3,2,0,1:T(8,128)S(1)} all-to-all(f32[2,64,32,256]{3,2,0,1:T(8,128)S(1)} %copy.160), channel_id=1, replica_groups=mesh['echo'=4,'space'=8] {'space'}, dimensions={1} | all-to-all | bytes 8388608 | tf_op jit(solution)/shard_map/all_to_all | solution.py:82
  1677.5 5.3 multiply_reduce_fusion.4
  1682.8 15.1 all-reduce
  1701.9 14.2 psum.54
  1731.3 3.4 add_bitcast_fusion.3
  1740.5 96.5 %all_to_all.155 = f32[2,8,256,256]{3,1,0,2:T(8,128)S(1)} all-to-all(f32[2,8,256,256]{3,1,0,2:T(8,128)S(1)} %copy.172), channel_id=1, replica_groups=mesh['echo'=4,'space'=8] {'space'}, dimensions={2} | all-to-all | bytes 8388608 | tf_op jit(solution)/shard_map/all_to_all | solution.py:79
  1858.9 96.5 %all_to_all.156 = f32[2,64,32,256]{3,2,0,1:T(8,128)S(1)} all-to-all(f32[2,64,32,256]{3,2,0,1:T(8,128)S(1)} %copy.174), channel_id=1, replica_groups=mesh['echo'=4,'space'=8] {'space'}, dimensions={1} | all-to-all | bytes 8388608 | tf_op jit(solution)/shard_map/all_to_all | solution.py:82
  1980.2 3.3 fusion.181
  1995.2 96.5 %all_to_all.157 = f32[2,8,256,256]{3,1,0,2:T(8,128)S(1)} all-to-all(f32[2,8,256,256]{3,1,0,2:T(8,128)S(1)} %copy.186), channel_id=1, replica_groups=mesh['echo'=4,'space'=8] {'space'}, dimensions={2} | all-to-all | bytes 8388608 | tf_op jit(solution)/shard_map/all_to_all | solution.py:79
  2113.6 96.5 %all_to_all.158 = f32[2,64,32,256]{3,2,0,1:T(8,128)S(1)} all-to-all(f32[2,64,32,256]{3,2,0,1:T(8,128)S(1)} %copy.188), channel_id=1, replica_groups=mesh['echo'=4,'space'=8] {'space'}, dimensions={1} | all-to-all | bytes 8388608 | tf_op jit(solution)/shard_map/all_to_all | solution.py:82
  2226.2 3.7 multiply_reduce_fusion.2
  2229.9 15.1 psum.55
  (191 shorter events, 307.6 us)
Async XLA Ops:
  7.2 811.0 %all-reduce.4.cloned.1.call-start = ((), (), s32[]{:S(2)}) async-start(), calls=%async_computation.10 | async-start | bytes 71303168 | tf_op jit(solution)/shard_map/psum | solution.py:107
  207.8 708.0 %copy-start.3 = (f32[8,256,256]{2,1,0:T(8,128)}, f32[8,256,256]{2,1,0:T(8,128)S(1)}, u32[]{:S(2)}) copy-start(f32[8,256,256]{2,1,0:T(8,128)S(1)} %fusion.121) | copy-start | bytes 6291460
  818.1 3.2 copy-start.14
  891.8 16.5 copy-start.10
  908.3 1.6 copy-start.6
  909.9 5.9 copy-start.13
  932.4 98.7 %all-to-all-start = ((f32[2,8,256,256]{3,1,0,2:T(8,128)}), f32[2,8,256,256]{3,1,0,2:T(8,128)}, u32[]{:S(2)}, u32[]{:S(2)}) async-start(f32[2,8,256,256]{3,1,0,2:T(8,128)} %copy.130), calls=%async_computation | async-start | bytes 8388608 | tf_op jit(solution)/shard_map/all_to_all | solution.py:79
  938.1 104.3 %copy-start = (f32[64,32,256]{2,0,1:T(8,128)}, f32[64,32,256]{2,0,1:T(8,128)S(1)}, u32[]{:S(2)}) copy-start(f32[64,32,256]{2,0,1:T(8,128)S(1)} %divide_subtract_fusion) | copy-start | bytes 6291460
  1167.8 2.9 copy-start.7
  1170.7 2.9 copy-start.4
  1295.2 2.2 copy-start.1
  1419.7 2.9 copy-start.11
  1717.4 2.2 copy-start.8
  1719.6 506.5 %copy-start.9 = (f32[8,256,256]{2,1,0:T(8,128)}, f32[8,256,256]{2,1,0:T(8,128)S(1)}, u32[]{:S(2)}) copy-start(f32[8,256,256]{2,1,0:T(8,128)S(1)} %multiply_add_fusion.2) | copy-start | bytes 6291460
  1719.6 3.0 copy-start.5
  1843.9 2.2 copy-start.2
  1968.5 2.9 copy-start.12
Sparse Core Ops, SparseCore 0:
  201.0 617.0 all-reduce.3
where the time goes:
time: 2260 us
  blocking collectives  913 us (40%)
  waiting for transfers between devices  703 us (31%)
  matrix products  317 us (14%)
  other arithmetic  259 us (11%)
  local copies, waits for them, and re-layouts  40.2 us (2%)
    psum x1, waiting for transfers between devices, on_device(): lax.psum((sums_real, sums_imag, power_part), 'echo')  610 us
    all_to_all x5, blocking collectives, full_dipole_map(): lax.all_to_all(pencils, 'space', split_axis=1, concat_axis=2, tiled=True)  483 us
    all_to_all x4, blocking collectives, full_dipole_map(): lax.all_to_all(complex_field, 'space', split_axis=2, concat_axis=1, tiled...  386 us
    dot_general x102, matrix products, contract_axis(): return jnp.einsum(pattern, operand, table, precision=lax.Precision.HIGHEST)  274 us
    unnamed x3, other arithmetic  96.5 us
    all_to_all x1, waiting for transfers between devices, full_dipole_map(): lax.all_to_all(complex_field, 'space', split_axis=2, concat_axis=1, tiled...  93 us
    sub x1, other arithmetic, on_device(): coil_contract(sens_real, image_imag) - coil_contract(sens_imag, image_real)  87.9 us
  transfers between devices with their start and end apart: 2, of which 2 were waited for; matrix products, arithmetic and copies ran while one was open for 0% of the time, Pallas kernels for 0%

commit v1 on v0

v1 whole, which is shorter than its diff:
```python
import functools
import math

import jax
import jax.numpy as jnp
import numpy as np
from jax import lax
from jax.experimental import pallas as pl
from jax.experimental.pallas import tpu as pltpu
from jax.sharding import PartitionSpec as P

power_floor = 0.5
tikhonov = 0.05


def coil_kernel(images_ref, sens_ref, out_ref, *, echoes, coils, rows, cols, row_step, col_step):
    def strip(start, col):
        at_rows = pl.ds(start, row_step)
        at_cols = pl.ds(col, col_step)
        sens_real = []
        sens_imag = []
        power = None
        for coil in range(coils):
            real = sens_ref[0, coil, 0, at_rows, at_cols].astype(jnp.float32)
            imag = sens_ref[1, coil, 0, at_rows, at_cols].astype(jnp.float32)
            sens_real.append(real)
            sens_imag.append(imag)
            square = real * real + imag * imag
            power = square if power is None else power + square
        out_ref[0, 2 * echoes, 0, at_rows, at_cols] = power
        for slot in range(echoes):
            total_real = None
            total_imag = None
            for coil in range(coils):
                real = images_ref[0, slot, coil, 0, at_rows, at_cols].astype(jnp.float32)
                imag = images_ref[1, slot, coil, 0, at_rows, at_cols].astype(jnp.float32)
                part_real = sens_real[coil] * real + sens_imag[coil] * imag
                part_imag = sens_real[coil] * imag - sens_imag[coil] * real
                total_real = part_real if total_real is None else total_real + part_real
                total_imag = part_imag if total_imag is None else total_imag + part_imag
            out_ref[0, slot, 0, at_rows, at_cols] = total_real
            out_ref[0, echoes + slot, 0, at_rows, at_cols] = total_imag

    @pl.loop(0, rows // row_step)
    def _(step):
        start = pl.multiple_of(step * row_step, row_step)
        for col in range(0, cols, col_step):
            strip(start, col)


def coil_sums(coil_images, sensitivities, parts, chunk, chunks):
    _, echoes, coils, depth, rows, cols = coil_images.shape
    part_depth = depth // parts
    chunk_rows = rows // chunks
    block_rows = min(64, chunk_rows)
    blocks = chunk_rows // block_rows
    col_step = 128 if cols % 128 == 0 else cols
    kernel = functools.partial(
        coil_kernel,
        echoes=echoes,
        coils=coils,
        rows=block_rows,
        cols=cols,
        row_step=min(16, block_rows),
        col_step=col_step,
    )
    voxels = depth * chunk_rows * cols
    first = chunk * blocks
    return pl.pallas_call(
        kernel,
        grid=(depth, blocks),
        in_specs=[
            pl.BlockSpec(
                (2, echoes, coils, 1, block_rows, cols), lambda z, b: (0, 0, 0, z, first + b, 0)
            ),
            pl.BlockSpec((2, coils, 1, block_rows, cols), lambda z, b: (0, 0, z, first + b, 0)),
        ],
        out_specs=pl.BlockSpec(
            (1, 2 * echoes + 1, 1, block_rows, cols),
            lambda z, b: (z // part_depth, 0, z % part_depth, b, 0),
        ),
        out_shape=jax.ShapeDtypeStruct(
            (parts, 2 * echoes + 1, part_depth, chunk_rows, cols), jnp.float32
        ),
        compiler_params=pltpu.CompilerParams(vmem_limit_bytes=32 << 20),
        cost_estimate=pl.CostEstimate(
            flops=voxels * echoes * coils * 8,
            bytes_accessed=voxels * (4 * coils * (echoes + 1) + 4 * (2 * echoes + 1)),
            transcendentals=0,
        ),
        name="coil_sums",
    )(coil_images, sensitivities)


def fit_kernel(slot_ref, sums_ref, mask_ref, field_ref, *, echoes):
    inverse_power = 1.0 / jnp.maximum(sums_ref[2 * echoes], power_floor)

    def ordered(k):
        slot = slot_ref[k]
        return sums_ref[slot] * inverse_power, sums_ref[echoes + slot] * inverse_power

    real, imag = ordered(0)
    power = real * real + imag * imag
    numerator = jnp.zeros_like(real)
    power_sum = jnp.zeros_like(real)
    for k in range(1, echoes):
        next_real, next_imag = ordered(k)
        next_power = next_real * next_real + next_imag * next_imag
        numerator = numerator + (real * next_imag - imag * next_real)
        power_sum = power_sum + 0.5 * (power + next_power)
        real, imag, power = next_real, next_imag, next_power
    field_ref[...] = mask_ref[...].astype(jnp.float32) * numerator / (1.0 + power_sum)


def fit_field(slot_of, sums, mask):
    fields, depth, rows, cols = sums.shape
    block_rows = min(32, rows)
    voxels = depth * rows * cols
    return pl.pallas_call(
        functools.partial(fit_kernel, echoes=(fields - 1) // 2),
        grid_spec=pltpu.PrefetchScalarGridSpec(
            num_scalar_prefetch=1,
            grid=(depth, rows // block_rows),
            in_specs=[
                pl.BlockSpec((fields, None, block_rows, cols), lambda z, b, s: (0, z, b, 0)),
                pl.BlockSpec((None, block_rows, cols), lambda z, b, s: (z, b, 0)),
            ],
            out_specs=pl.BlockSpec((None, block_rows, cols), lambda z, b, s: (z, b, 0)),
        ),
        out_shape=jax.ShapeDtypeStruct((depth, rows, cols), jnp.float32),
        cost_estimate=pl.CostEstimate(
            flops=voxels * 100, bytes_accessed=voxels * 4 * (fields + 2), transcendentals=0
        ),
        name="fit_field",
    )(slot_of, sums, mask)


def signed_frequency(positions, length):
    shifted = jnp.where(positions < length // 2, positions, positions - length)
    return shifted.astype(jnp.float32) / length


def kernel_values(z_index, x_index, y_index, depth_len, rows_len, cols_len):
    freq_z = signed_frequency(z_index, depth_len)[:, None, None]
    freq_x = signed_frequency(x_index, rows_len)[None, :, None]
    freq_y = signed_frequency(y_index, cols_len)[None, None, :]
    anchor = (
        (z_index[:, None, None] == 0)
        & (x_index[None, :, None] == 0)
        & (y_index[None, None, :] == 0)
    ).astype(jnp.float32)
    total = freq_z * freq_z + freq_x * freq_x + freq_y * freq_y
    return 1.0 / 3.0 - freq_z * freq_z / (total + anchor)


def hartley_table(length):
    index = np.arange(length)
    radians = 2.0 * math.pi / length * (index[:, None] * index[None, :] % length)
    return jnp.asarray(
        ((np.cos(radians) + np.sin(radians)) / math.sqrt(length)).astype(np.float32)
    )


def on_device(coil_images, sensitivities, mask, echo_order):
    depth, rows, cols = mask.shape
    echo_parts = lax.axis_size("echo")
    split = depth % echo_parts == 0
    parts = echo_parts if split else 1
    axes = ("space", "echo") if split else ("space",)
    part_depth = depth // parts
    count = lax.axis_size("space") * parts
    full_depth = depth * lax.axis_size("space")
    pencil_rows = rows // count
    echoes = echo_order.shape[0]

    numbers = jnp.arange(echoes, dtype=jnp.int32)
    slot_of = jnp.sum(
        jnp.where(echo_order[None, :] == numbers[:, None], numbers[None, :], 0), axis=1
    ).astype(jnp.int32)
    own_mask = mask
    if split:
        own_mask = lax.dynamic_slice_in_dim(
            mask, lax.axis_index("echo") * part_depth, part_depth, 0
        )

    chunks = 4
    chunk_rows = rows // chunks
    fields = []
    for chunk in range(chunks):
        sums = coil_sums(coil_images, sensitivities, parts, chunk, chunks)
        if split:
            sums = lax.psum_scatter(sums, "echo", scatter_dimension=0, tiled=True)
        else:
            sums = lax.psum(sums, "echo")
        chunk_mask = lax.slice_in_dim(own_mask, chunk * chunk_rows, (chunk + 1) * chunk_rows, axis=1)
        fields.append(fit_field(slot_of, sums[0], chunk_mask))
    field = jnp.concatenate(fields, axis=1)

    def spread(values):
        return lax.all_gather(values, "echo", axis=0, tiled=True) if split else values

    place = lax.axis_index("space")
    if split:
        place = place * parts + lax.axis_index("echo")
    dipole = kernel_values(
        jnp.arange(full_depth, dtype=jnp.int32),
        place * pencil_rows + jnp.arange(pencil_rows, dtype=jnp.int32),
        jnp.arange(cols, dtype=jnp.int32),
        full_depth,
        rows,
        cols,
    )
    weights = own_mask.astype(jnp.float32)
    table_z = hartley_table(full_depth)
    table_x = hartley_table(rows)
    table_y = hartley_table(cols)
    exact = functools.partial(jnp.einsum, precision=lax.Precision.HIGHEST)

    def forward(values):
        values = exact("zxy,yl->zxl", values, table_y)
        values = exact("zxl,xk->zkl", values, table_x)
        pencils = lax.all_to_all(values, axes, split_axis=1, concat_axis=0, tiled=True)
        return exact("zkl,zm->mkl", pencils, table_z)

    def backward(spectrum):
        pencils = exact("mkl,mz->zkl", spectrum, table_z)
        values = lax.all_to_all(pencils, axes, split_axis=0, concat_axis=1, tiled=True)
        values = exact("zkl,kx->zxl", values, table_x)
        return exact("zxl,ly->zxy", values, table_y)

    field_map = spread(field)
    right_hat = dipole * forward(weights * field)
    filtered = backward(dipole * right_hat)
    masked = weights * filtered
    old_norm, inner = lax.psum(
        (jnp.sum(right_hat * right_hat), jnp.sum(masked * filtered)), axes
    )
    step_first = old_norm / (inner + tikhonov * old_norm)
    image_hat = dipole * forward(masked) + tikhonov * right_hat
    residual_hat = right_hat - step_first * image_hat
    new_norm, cross = lax.psum(
        (jnp.sum(residual_hat * residual_hat), jnp.sum(residual_hat * right_hat)), axes
    )
    ratio = new_norm / old_norm
    filtered_next = backward(dipole * residual_hat) + ratio * filtered
    direction_norm = new_norm + 2.0 * ratio * cross + ratio * ratio * old_norm
    inner_next = lax.psum(jnp.sum(weights * filtered_next * filtered_next), axes)
    step_second = new_norm / (inner_next + tikhonov * direction_norm)
    first_part = spread(backward(right_hat))
    second_part = spread(backward(residual_hat))
    susceptibility = (step_first + step_second * ratio) * first_part + step_second * second_part
    return (field_map, susceptibility)


def solution(mesh):
    placed = (
        P(None, None, "echo", "space", None, None),
        P(None, "echo", "space", None, None),
        P("space", None, None),
        P(),
    )
    return jax.shard_map(
        on_device,
        mesh=mesh,
        in_specs=placed,
        out_specs=(P("space", None, None), P("space", None, None)),
        check_vma=False,
    )
```

time: 2260 us -> 657 us (0.29)
  blocking collectives: 913 us -> 146 us
  waiting for transfers between devices: 703 us -> 346 us
  matrix products: 317 us -> 22.9 us
  other arithmetic: 259 us -> 5.57 us
  Pallas kernels: 0 us -> 62 us
    all_to_all x9 -> x1, blocking collectives: 869 us -> 20.2 us  [backward(): lax.all_to_all(pencils, axes, split_axis=0, concat_axis=1, tiled=True)]
    psum x1 -> x0, waiting for transfers between devices: 610 us -> none  [on_device(): lax.psum((sums_real, sums_imag, power_part), 'echo')]
    unnamed x1 -> x11, waiting for transfers between devices: 0.02 us -> 305 us
    dot_general x104 -> x18, matrix products: 317 us -> 22.9 us  [the longest x4 6.91 us: backward(): return exact('zxl,ly->zxy', values, table_y)]
    unnamed x3 -> x0, other arithmetic: 96.5 us -> none
    sub x2 -> x0, other arithmetic: 88.6 us -> none  [the longest x1 87.9 us: on_device(): coil_contract(sens_real, image_imag) - coil_contract(sens_imag, image_real)]
    psum x3, blocking collectives: 44.5 us -> 125 us  [the longest x1 43.2 us: on_device(): lax.psum((jnp.sum(residual_hat * residual_hat), jnp.sum(residual_hat * ri...]
    pallas_call x0 -> x8, Pallas kernels: none -> 62 us  [the longest x4 44.8 us: coil_sums(): pl.pallas_call(kernel, grid=(depth, blocks), in_specs=[pl.BlockSpec((2, e...]
  transfers between devices with their start and end apart: 2 -> 12, of which waited for: 2 -> 7; matrix products, arithmetic and copies ran while one was open for 0% -> 4% of each run, Pallas kernels for 0% -> 7%
where the time goes in v1:
time: 657 us; the launch traced here: 655 us
  waiting for transfers between devices  346 us (53%)
  blocking collectives  146 us (22%)
  Pallas kernels  62 us (9%)
  local copies, waits for them, and re-layouts  36.5 us (6%)
  matrix products  22.9 us (3%)
  between operations  20.9 us (3%)
  starting transfers between devices  15.5 us (2%)
    unnamed x11, waiting for transfers between devices  305 us
    pallas_call x4, Pallas kernels, coil_sums(): pl.pallas_call(kernel, grid=(depth, blocks), in_specs=[pl.BlockSpec((2, e...  44.8 us
    psum x1, blocking collectives, on_device(): lax.psum((jnp.sum(residual_hat * residual_hat), jnp.sum(residual_hat * ri...  43.2 us
    psum x1, blocking collectives, on_device(): lax.psum((jnp.sum(right_hat * right_hat), jnp.sum(masked * filtered)), axes)  43 us
    psum x1, blocking collectives, on_device(): lax.psum(jnp.sum(weights * filtered_next * filtered_next), axes)  39.2 us
    unnamed x39, local copies, waits for them, and re-layouts  30 us
    all_to_all x3, waiting for transfers between devices, backward(): lax.all_to_all(pencils, axes, split_axis=0, concat_axis=1, tiled=True)  26.4 us
    all_to_all x1, blocking collectives, backward(): lax.all_to_all(pencils, axes, split_axis=0, concat_axis=1, tiled=True)  20.2 us
  transfers between devices with their start and end apart: 12, of which 7 were waited for; matrix products, arithmetic and copies ran while one was open for 4% of the time, Pallas kernels for 7%

profile of v1, /device:TPU:0, one launch (start us, length us, event | category | flops | bytes accessed | tf_op | source)
XLA Modules:
  0.0 655.4 jit_solution(13884404490159300176)
XLA Ops:
  7.2 3.4 copy-done
  10.6 11.0 %coil_sums.4 = f32[4,17,2,64,256]{4,3,2,1,0:T(8,128)S(1)} custom-call(bf16[2,8,4,8,256,256]{5,4,3,2,1,0:T(8,128)(2,1)} %images_ref.7, bf16[2,4,8,256,256]{4,3,2,1,0:T(8,128)(2,1)S(1)} %copy-done), custom_call_target="tpu_custom_call" | custom-call | flops 33554432 | bytes 27787264 | tf_op jit(solution)/shard_map/coil_sums/pallas_call | solution.py:69
  21.6 3.4 copy-done.4
  25.1 3.4 copy-done.1
  28.5 11.3 %coil_sums.5 = f32[4,17,2,64,256]{4,3,2,1,0:T(8,128)S(1)} custom-call(bf16[2,8,4,8,256,256]{5,4,3,2,1,0:T(8,128)(2,1)} %images_ref.7, bf16[2,4,8,256,256]{4,3,2,1,0:T(8,128)(2,1)S(1)} %copy-done.1), custom_call_target="tpu_custom_call" | custom-call | flops 33554432 | bytes 27787264 | tf_op jit(solution)/shard_map/coil_sums/pallas_call | solution.py:69
  39.8 3.5 copy-done.5
  43.4 3.6 copy-done.2
  47.0 11.4 %coil_sums.6 = f32[4,17,2,64,256]{4,3,2,1,0:T(8,128)S(1)} custom-call(bf16[2,8,4,8,256,256]{5,4,3,2,1,0:T(8,128)(2,1)} %images_ref.7, bf16[2,4,8,256,256]{4,3,2,1,0:T(8,128)(2,1)S(1)} %copy-done.2), custom_call_target="tpu_custom_call" | custom-call | flops 33554432 | bytes 27787264 | tf_op jit(solution)/shard_map/coil_sums/pallas_call | solution.py:69
  58.4 3.4 copy-done.6
  61.9 3.5 copy-done.3
  65.4 11.1 %coil_sums.7 = f32[4,17,2,64,256]{4,3,2,1,0:T(8,128)S(1)} custom-call(bf16[2,8,4,8,256,256]{5,4,3,2,1,0:T(8,128)(2,1)} %images_ref.7, bf16[2,4,8,256,256]{4,3,2,1,0:T(8,128)(2,1)S(1)} %copy-done.3), custom_call_target="tpu_custom_call" | custom-call | flops 33554432 | bytes 27787264 | tf_op jit(solution)/shard_map/coil_sums/pallas_call | solution.py:69
  76.5 3.4 copy-done.7
  82.4 36.2 %reduce-scatter.13.cloned.1.call-done = f32[1,17,2,64,256]{4,3,2,1,0:T(8,128)} async-done(((f32[4,17,2,64,256]{4,3,2,1,0:T(8,128)}), f32[1,17,2,64,256]{4,3,2,1,0:T(8,128)}) %reduce-scatter.13.cloned.1.call-update) | async-done | bytes 2228240
  118.6 4.3 fit_field.4
  122.9 89.6 %reduce-scatter.15.cloned.1.call-done = f32[1,17,2,64,256]{4,3,2,1,0:T(8,128)} async-done(((f32[4,17,2,64,256]{4,3,2,1,0:T(8,128)}), f32[1,17,2,64,256]{4,3,2,1,0:T(8,128)}) %reduce-scatter.15.cloned.1.call-update) | async-done | bytes 2228240
  212.5 4.3 fit_field.5
  216.7 89.6 %reduce-scatter.17.cloned.1.call-done = f32[1,17,2,64,256]{4,3,2,1,0:T(8,128)} async-done(((f32[4,17,2,64,256]{4,3,2,1,0:T(8,128)}), f32[1,17,2,64,256]{4,3,2,1,0:T(8,128)}) %reduce-scatter.17.cloned.1.call-update) | async-done | bytes 2228240
  306.4 4.4 fit_field.6
  310.8 89.3 %reduce-scatter.19.cloned.1.call-done = f32[1,17,2,64,256]{4,3,2,1,0:T(8,128)} async-done(((f32[4,17,2,64,256]{4,3,2,1,0:T(8,128)}), f32[1,17,2,64,256]{4,3,2,1,0:T(8,128)}) %reduce-scatter.19.cloned.1.call-update) | async-done | bytes 2228240
  400.1 4.3 fit_field.7
  407.6 4.6 all-to-all-start
  413.3 15.1 %all-to-all-done = f32[2,256,256]{2,0,1:T(2,128)S(1)} async-done(((f32[2,256,256]{2,0,1:T(2,128)}), f32[2,256,256]{2,0,1:T(2,128)S(1)}, u32[]{:S(2)}, u32[]{:S(2)}) %all-to-all-start) | async-done | bytes 524320 | tf_op jit(solution)/shard_map/all_to_all | solution.py:222
  431.8 2.6 all-to-all-start.1
  436.1 14.5 %all-to-all-done.1 = f32[64,8,256]{2,1,0:T(8,128)S(1)} async-done(((f32[64,8,256]{2,1,0:T(8,128)}), f32[64,8,256]{2,1,0:T(8,128)S(1)}, u32[]{:S(2)}, u32[]{:S(2)}) %all-to-all-start.1) | async-done | bytes 524320 | tf_op jit(solution)/shard_map/all_to_all | solution.py:227
  450.7 2.6 all-to-all-start.4
  457.7 11.9 %all-to-all-done.4 = f32[64,8,256]{2,1,0:T(8,128)S(1)} async-done(((f32[64,8,256]{2,1,0:T(8,128)}), f32[64,8,256]{2,1,0:T(8,128)S(1)}, u32[]{:S(2)}, u32[]{:S(2)}) %all-to-all-start.4) | async-done | bytes 524320 | tf_op jit(solution)/shard_map/all_to_all | solution.py:227
  475.0 2.6 all-to-all-start.2
  477.7 43.0 %all-reduce.5 = (f32[]{:T(128)}, f32[]{:T(128)}) all-reduce(f32[]{:T(128)} %get-tuple-element.12, f32[]{:T(128)} %get-tuple-element.14), channel_id=1, replica_groups=mesh['echo'=4,'space'=8] {'space','echo'}, use_global_device_ids=true, to_apply=%region_6.7 | all-reduce | flops 2 | bytes 16 | tf_op jit(solution)/shard_map/psum | solution.py:235
  526.2 20.2 %all_to_all.108 = f32[64,8,256]{2,1,0:T(8,128)S(1)} all-to-all(f32[64,8,256]{2,1,0:T(8,128)S(1)} %copy.81), channel_id=1, replica_groups=mesh['echo'=4,'space'=8] {'space','echo'}, dimensions={0} | all-to-all | bytes 1048576 | tf_op jit(solution)/shard_map/all_to_all | solution.py:227
  553.7 43.2 %psum.37 = f32[]{:T(128)} all-reduce(f32[]{:T(128)} %get-tuple-element.3), channel_id=1, replica_groups=mesh['echo'=4,'space'=8] {'space','echo'}, use_global_device_ids=true, to_apply=%region_10.11 | all-reduce | flops 1 | bytes 8 | tf_op jit(solution)/shard_map/psum | solution.py:241
  601.6 39.2 %all-reduce.4 = (f32[]{:T(128)}, f32[]{:T(128)}) all-reduce(f32[]{:T(128)} %fusion.3, f32[]{:T(128)} %get-tuple-element.2), channel_id=1, replica_groups=mesh['echo'=4,'space'=8] {'space','echo'}, use_global_device_ids=true, to_apply=%region_12.13 | all-reduce | flops 2 | bytes 16 | tf_op jit(solution)/shard_map/psum | solution.py:247
  643.3 4.0 multiply_add_fusion
  (88 shorter events, 36.6 us)
Async XLA Ops:
  7.2 111.4 %reduce-scatter.13.cloned.1.call-start = ((), (), s32[]{:S(2)}) async-start(), calls=%async_computation.13 | async-start | bytes 11141120
  7.2 3.4 copy-start
  21.6 3.4 copy-start.4
  25.0 187.4 %reduce-scatter.15.cloned.1.call-start = ((), (), s32[]{:S(2)}) async-start(), calls=%async_computation.14 | async-start | bytes 11141120
  25.1 3.4 copy-start.1
  39.8 3.5 copy-start.5
  43.3 263.0 %reduce-scatter.17.cloned.1.call-start = ((), (), s32[]{:S(2)}) async-start(), calls=%async_computation.15 | async-start | bytes 11141120
  43.4 3.7 copy-start.2
  58.4 3.5 copy-start.6
  61.9 338.2 %reduce-scatter.19.cloned.1.call-start = ((), (), s32[]{:S(2)}) async-start(), calls=%async_computation.16 | async-start | bytes 11141120
  61.9 3.5 copy-start.3
  76.5 3.4 copy-start.7
  80.0 0.7 copy-start.17
  80.0 1.6 copy-start.9
  306.3 98.0 %copy-start.8 = (f32[256,256,1]{1,0,2:T(8,128)S(1)}, f32[256,256,1]{1,0,2:T(8,128)}, u32[]{:S(2)}) copy-start(f32[256,256,1]{1,0,2:T(8,128)} %constant.75) | copy-start | bytes 786436
  306.3 98.0 %copy-start.11 = (f32[2,64,256]{2,1,0:T(8,128)S(1)}, f32[2,64,256]{2,1,0:T(8,128)}, u32[]{:S(2)}) copy-start(f32[2,64,256]{2,1,0:T(8,128)} %fit_field.4) | copy-start | bytes 393220
  306.4 98.0 %copy-start.12 = (f32[2,64,256]{2,1,0:T(8,128)S(1)}, f32[2,64,256]{2,1,0:T(8,128)}, u32[]{:S(2)}) copy-start(f32[2,64,256]{2,1,0:T(8,128)} %fit_field.5) | copy-start | bytes 393220
  310.8 93.6 %copy-start.13 = (f32[2,64,256]{2,1,0:T(8,128)S(1)}, f32[2,64,256]{2,1,0:T(8,128)}, u32[]{:S(2)}) copy-start(f32[2,64,256]{2,1,0:T(8,128)} %fit_field.6) | copy-start | bytes 393220
  406.0 6.4 copy-start.14
  407.6 20.9 %copy-start.18 = (f32[64,64,1]{0,1,2:T(8,128)S(1)}, f32[64,64,1]{0,1,2:T(8,128)}, u32[]{:S(2)}) copy-start(f32[64,64,1]{0,1,2:T(8,128)} %constant.74) | copy-start | bytes 49156
  407.6 20.8 %all-to-all-start = ((f32[2,256,256]{2,0,1:T(2,128)}), f32[2,256,256]{2,0,1:T(2,128)S(1)}, u32[]{:S(2)}, u32[]{:S(2)}) async-start(f32[2,256,256]{2,0,1:T(2,128)} %copy.62), calls=%async_computation | async-start | bytes 1048576 | tf_op jit(solution)/shard_map/all_to_all | solution.py:222
  412.2 186.7 %all-gather.4.cloned.1.call-start = ((), (), s32[]{:S(2)}) async-start(), calls=%async_computation.10 | async-start | bytes 2621440 | tf_op jit(solution)/shard_map/all_gather | solution.py:200
  413.3 16.7 %copy-start.16 = (f32[64,64,1]{0,1,2:T(8,128)S(1)}, f32[64,64,1]{0,1,2:T(8,128)}, u32[]{:S(2)}) copy-start(f32[64,64,1]{0,1,2:T(8,128)} %constant.76) | copy-start | bytes 49156
  429.9 4.5 copy-start.15
  431.8 18.9 %all-to-all-start.1 = ((f32[64,8,256]{2,1,0:T(8,128)}), f32[64,8,256]{2,1,0:T(8,128)S(1)}, u32[]{:S(2)}, u32[]{:S(2)}) async-start(f32[64,8,256]{2,1,0:T(8,128)} %copy.65), calls=%async_computation.1 | async-start | bytes 1048576 | tf_op jit(solution)/shard_map/all_to_all | solution.py:227
  450.7 18.9 %all-to-all-start.4 = ((f32[64,8,256]{2,1,0:T(8,128)}), f32[64,8,256]{2,1,0:T(8,128)S(1)}, u32[]{:S(2)}, u32[]{:S(2)}) async-start(f32[64,8,256]{2,1,0:T(8,128)} %copy.77), calls=%async_computation.4 | async-start | bytes 1048576 | tf_op jit(solution)/shard_map/all_to_all | solution.py:227
  453.3 189.9 %all-gather.6.cloned.1.call-start = ((), (), s32[]{:S(2)}) async-start(), calls=%async_computation.11 | async-start | bytes 2621440 | tf_op jit(solution)/shard_map/all_gather | solution.py:200
  475.0 47.7 %all-to-all-start.2 = ((f32[2,256,256]{2,0,1:T(2,128)}), f32[2,256,256]{2,0,1:T(2,128)S(1)}, u32[]{:S(2)}, u32[]{:S(2)}) async-start(f32[2,256,256]{2,0,1:T(2,128)} %copy.70), calls=%async_computation.2 | async-start | bytes 1048576 | tf_op jit(solution)/shard_map/all_to_all | solution.py:222
  477.6 165.6 %all-gather.8.cloned.1.call-start = ((), (), s32[]{:S(2)}) async-start(), calls=%async_computation.12 | async-start | bytes 2621440 | tf_op jit(solution)/shard_map/all_gather | solution.py:200
  551.1 47.8 %all-to-all-start.3 = ((f32[64,8,256]{2,1,0:T(8,128)}), f32[64,8,256]{2,1,0:T(8,128)S(1)}, u32[]{:S(2)}, u32[]{:S(2)}) async-start(f32[64,8,256]{2,1,0:T(8,128)} %copy.73), calls=%async_computation.3 | async-start | bytes 1048576 | tf_op jit(solution)/shard_map/all_to_all | solution.py:227
  643.2 4.0 copy-start.10
Sparse Core Ops, SparseCore 0:
  25.1 93.3 reduce-scatter.12
  121.7 90.6 reduce-scatter.14
  215.6 90.6 reduce-scatter.16
  309.3 90.6 reduce-scatter.18
  415.1 40.1 all-gather.3
  472.5 38.9 all-gather.5
  549.4 38.3 all-gather.7

commit v2 on v1

--- a/solution.py
+++ b/solution.py
@@ -13,7 +13,7 @@
 tikhonov = 0.05
 
 
-def coil_kernel(images_ref, sens_ref, out_ref, *, echoes, coils, rows, cols, row_step, col_step):
+def coil_kernel(place_ref, images_ref, sens_ref, out_ref, *, echoes, coils, rows, cols, row_step, col_step):
     def strip(start, col):
         at_rows = pl.ds(start, row_step)
         at_cols = pl.ds(col, col_step)
@@ -48,9 +48,8 @@
             strip(start, col)
 
 
-def coil_sums(coil_images, sensitivities, parts, chunk, chunks):
+def coil_sums(coil_images, sensitivities, place, groups, part_depth, chunk, chunks):
     _, echoes, coils, depth, rows, cols = coil_images.shape
-    part_depth = depth // parts
     chunk_rows = rows // chunks
     block_rows = min(64, chunk_rows)
     blocks = chunk_rows // block_rows
@@ -64,20 +63,32 @@
         row_step=min(16, block_rows),
         col_step=col_step,
     )
-    voxels = depth * chunk_rows * cols
+    parts = len(groups)
+    stride = groups[1] - groups[0] if parts > 1 else 0
+    voxels = parts * part_depth * chunk_rows * cols
     first = chunk * blocks
+
+    def plane(i, z, place_ref):
+        return (place_ref[0] ^ (groups[0] + stride * i)) * part_depth + z
+
     return pl.pallas_call(
         kernel,
-        grid=(depth, blocks),
-        in_specs=[
-            pl.BlockSpec(
-                (2, echoes, coils, 1, block_rows, cols), lambda z, b: (0, 0, 0, z, first + b, 0)
+        grid_spec=pltpu.PrefetchScalarGridSpec(
+            num_scalar_prefetch=1,
+            grid=(parts, part_depth, blocks),
+            in_specs=[
+                pl.BlockSpec(
+                    (2, echoes, coils, 1, block_rows, cols),
+                    lambda i, z, b, p: (0, 0, 0, plane(i, z, p), first + b, 0),
+                ),
+                pl.BlockSpec(
+                    (2, coils, 1, block_rows, cols),
+                    lambda i, z, b, p: (0, 0, plane(i, z, p), first + b, 0),
+                ),
+            ],
+            out_specs=pl.BlockSpec(
+                (1, 2 * echoes + 1, 1, block_rows, cols), lambda i, z, b, p: (i, 0, z, b, 0)
             ),
-            pl.BlockSpec((2, coils, 1, block_rows, cols), lambda z, b: (0, 0, z, first + b, 0)),
-        ],
-        out_specs=pl.BlockSpec(
-            (1, 2 * echoes + 1, 1, block_rows, cols),
-            lambda z, b: (z // part_depth, 0, z % part_depth, b, 0),
         ),
         out_shape=jax.ShapeDtypeStruct(
             (parts, 2 * echoes + 1, part_depth, chunk_rows, cols), jnp.float32
@@ -89,15 +100,23 @@
             transcendentals=0,
         ),
         name="coil_sums",
-    )(coil_images, sensitivities)
-
-
-def fit_kernel(slot_ref, sums_ref, mask_ref, field_ref, *, echoes):
-    inverse_power = 1.0 / jnp.maximum(sums_ref[2 * echoes], power_floor)
+    )(place, coil_images, sensitivities)
+
+
+def fit_kernel(slot_ref, *refs, echoes):
+    *term_refs, mask_ref, field_ref = refs
+
+    def total(index):
+        value = term_refs[0][index]
+        for term_ref in term_refs[1:]:
+            value = value + term_ref[index]
+        return value
+
+    inverse_power = 1.0 / jnp.maximum(total(2 * echoes), power_floor)
 
     def ordered(k):
         slot = slot_ref[k]
-        return sums_ref[slot] * inverse_power, sums_ref[echoes + slot] * inverse_power
+        return total(slot) * inverse_power, total(echoes + slot) * inverse_power
 
     real, imag = ordered(0)
     power = real * real + imag * imag
@@ -112,27 +131,30 @@
     field_ref[...] = mask_ref[...].astype(jnp.float32) * numerator / (1.0 + power_sum)
 
 
-def fit_field(slot_of, sums, mask):
-    fields, depth, rows, cols = sums.shape
+def fit_field(slot_of, terms, mask):
+    _, fields, depth, rows, cols = terms[0].shape
     block_rows = min(32, rows)
     voxels = depth * rows * cols
+    term_spec = pl.BlockSpec(
+        (None, fields, None, block_rows, cols), lambda z, b, s: (0, 0, z, b, 0)
+    )
+    plane_spec = pl.BlockSpec((None, block_rows, cols), lambda z, b, s: (z, b, 0))
     return pl.pallas_call(
         functools.partial(fit_kernel, echoes=(fields - 1) // 2),
         grid_spec=pltpu.PrefetchScalarGridSpec(
             num_scalar_prefetch=1,
             grid=(depth, rows // block_rows),
-            in_specs=[
-                pl.BlockSpec((fields, None, block_rows, cols), lambda z, b, s: (0, z, b, 0)),
-                pl.BlockSpec((None, block_rows, cols), lambda z, b, s: (z, b, 0)),
-            ],
-            out_specs=pl.BlockSpec((None, block_rows, cols), lambda z, b, s: (z, b, 0)),
+            in_specs=[term_spec] * len(terms) + [plane_spec],
+            out_specs=plane_spec,
         ),
         out_shape=jax.ShapeDtypeStruct((depth, rows, cols), jnp.float32),
         cost_estimate=pl.CostEstimate(
-            flops=voxels * 100, bytes_accessed=voxels * 4 * (fields + 2), transcendentals=0
+            flops=voxels * 100,
+            bytes_accessed=voxels * 4 * (fields * len(terms) + 2),
+            transcendentals=0,
         ),
         name="fit_field",
-    )(slot_of, sums, mask)
+    )(slot_of, *terms, mask)
 
 
 def signed_frequency(positions, length):
@@ -183,17 +205,36 @@
             mask, lax.axis_index("echo") * part_depth, part_depth, 0
         )
 
-    chunks = 4
+    chunks = 8
     chunk_rows = rows // chunks
+    echo_place = lax.axis_index("echo").astype(jnp.int32).reshape(1)
+    origin = jnp.zeros((1,), jnp.int32)
+    pairwise = split and echo_parts == 4
     fields = []
     for chunk in range(chunks):
-        sums = coil_sums(coil_images, sensitivities, parts, chunk, chunks)
-        if split:
-            sums = lax.psum_scatter(sums, "echo", scatter_dimension=0, tiled=True)
+        if pairwise:
+            near, far = ((1, 2), (2, 1))[chunk % 2]
+
+            def partner(values, offset):
+                return lax.ppermute(values, "echo", [(e, e ^ offset) for e in range(4)])
+
+            place = (part_depth, chunk, chunks)
+            sent = coil_sums(coil_images, sensitivities, echo_place, (near, 3), *place)
+            arrived = partner(sent, near)
+            kept = coil_sums(coil_images, sensitivities, echo_place, (0, far), *place)
+            terms = (kept, arrived, partner(kept[1:] + arrived[1:], far))
         else:
-            sums = lax.psum(sums, "echo")
+            groups = tuple(range(parts))
+            sums = coil_sums(
+                coil_images, sensitivities, origin, groups, part_depth, chunk, chunks
+            )
+            if split:
+                sums = lax.psum_scatter(sums, "echo", scatter_dimension=0, tiled=True)
+            else:
+                sums = lax.psum(sums, "echo")
+            terms = (sums,)
         chunk_mask = lax.slice_in_dim(own_mask, chunk * chunk_rows, (chunk + 1) * chunk_rows, axis=1)
-        fields.append(fit_field(slot_of, sums[0], chunk_mask))
+        fields.append(fit_field(slot_of, terms, chunk_mask))
     field = jnp.concatenate(fields, axis=1)
 
     def spread(values):
@@ -228,23 +269,33 @@
         values = exact("zkl,kx->zxl", values, table_x)
         return exact("zxl,ly->zxy", values, table_y)
 
+    def totals(*values):
+        row = jnp.pad(jnp.stack(values), (0, 128 - len(values)))
+        copies = jnp.broadcast_to(row, (count, 1, 128))
+        return jnp.sum(
+            lax.all_to_all(copies, axes, split_axis=0, concat_axis=0, tiled=True), axis=(0, 1)
+        )
+
     field_map = spread(field)
     right_hat = dipole * forward(weights * field)
     filtered = backward(dipole * right_hat)
     masked = weights * filtered
-    old_norm, inner = lax.psum(
-        (jnp.sum(right_hat * right_hat), jnp.sum(masked * filtered)), axes
-    )
+    sums = totals(jnp.sum(right_hat * right_hat), jnp.sum(masked * filtered))
+    old_norm, inner = sums[0], sums[1]
     step_first = old_norm / (inner + tikhonov * old_norm)
     image_hat = dipole * forward(masked) + tikhonov * right_hat
     residual_hat = right_hat - step_first * image_hat
-    new_norm, cross = lax.psum(
-        (jnp.sum(residual_hat * residual_hat), jnp.sum(residual_hat * right_hat)), axes
-    )
+    filtered_next = backward(dipole * residual_hat)
+    sums = totals(
+        jnp.sum(residual_hat * residual_hat),
+        jnp.sum(residual_hat * right_hat),
+        jnp.sum(weights * filtered_next * filtered_next),
+        jnp.sum(masked * filtered_next),
+    )
+    new_norm = sums[0]
     ratio = new_norm / old_norm
-    filtered_next = backward(dipole * residual_hat) + ratio * filtered
-    direction_norm = new_norm + 2.0 * ratio * cross + ratio * ratio * old_norm
-    inner_next = lax.psum(jnp.sum(weights * filtered_next * filtered_next), axes)
+    direction_norm = new_norm + 2.0 * ratio * sums[1] + ratio * ratio * old_norm
+    inner_next = sums[2] + 2.0 * ratio * sums[3] + ratio * ratio * inner
     step_second = new_norm / (inner_next + tikhonov * direction_norm)
     first_part = spread(backward(right_hat))
     second_part = spread(backward(residual_hat))

time: 657 us -> 491 us (0.75)
  waiting for transfers between devices: 346 us -> 227 us
  blocking collectives: 146 us -> 36.9 us
  Pallas kernels: 62 us -> 100 us
  starting transfers between devices: 15.5 us -> 40.4 us
  local copies, waits for them, and re-layouts: 36.5 us -> 18 us
  other arithmetic: 5.57 us -> 21.3 us
    unnamed x11 -> x3, waiting for transfers between devices: 305 us -> 0.31 us
    ppermute x0 -> x16, waiting for transfers between devices: none -> 164 us  [partner(): return lax.ppermute(values, 'echo', [(e, e ^ offset) for e in range(4)])]
    psum x3 -> x0, blocking collectives: 125 us -> none  [the longest x1 43.2 us: on_device(): lax.psum((jnp.sum(residual_hat * residual_hat), jnp.sum(residual_hat * ri...]
    pallas_call x4 -> x16, Pallas kernels: 44.8 us -> 72.7 us  [coil_sums(): pl.pallas_call(kernel, grid_spec=pltpu.PrefetchScalarGridSpec(num_scalar_...]
    unnamed x39 -> x70, local copies, waits for them, and re-layouts: 30 us -> 7.91 us
    ppermute x0 -> x16, starting transfers between devices: none -> 20.4 us  [partner(): return lax.ppermute(values, 'echo', [(e, e ^ offset) for e in range(4)])]
    all_to_all x1 -> x2, blocking collectives: 20.2 us -> 36.9 us  [backward(): lax.all_to_all(pencils, axes, split_axis=0, concat_axis=1, tiled=True)]
    all_to_all x2, waiting for transfers between devices: 15.2 us -> 29.2 us  [forward(): lax.all_to_all(values, axes, split_axis=1, concat_axis=0, tiled=True)]
  transfers between devices with their start and end apart: 12 -> 25, of which waited for: 7 -> 16; matrix products, arithmetic and copies ran while one was open for 4% -> 10% of each run, Pallas kernels for 7% -> 19%
where the time goes in v2:
time: 491 us; the launch traced here: 488 us
  waiting for transfers between devices  227 us (46%)
  Pallas kernels  100 us (20%)
  starting transfers between devices  40.4 us (8%)
  blocking collectives  36.9 us (8%)
  matrix products  22.2 us (5%)
  between operations  22 us (4%)
  other arithmetic  21.3 us (4%)
  local copies, waits for them, and re-layouts  18 us (4%)
    ppermute x16, waiting for transfers between devices, partner(): return lax.ppermute(values, 'echo', [(e, e ^ offset) for e in range(4)])  164 us
    pallas_call x16, Pallas kernels, coil_sums(): pl.pallas_call(kernel, grid_spec=pltpu.PrefetchScalarGridSpec(num_scalar_...  72.7 us
    all_to_all x2, blocking collectives, backward(): lax.all_to_all(pencils, axes, split_axis=0, concat_axis=1, tiled=True)  36.9 us
    all_to_all x2, waiting for transfers between devices, forward(): lax.all_to_all(values, axes, split_axis=1, concat_axis=0, tiled=True)  29.2 us
    pallas_call x8, Pallas kernels, fit_field(): pl.pallas_call(functools.partial(fit_kernel, echoes=(fields - 1) // 2), g...  27.5 us
    all_to_all x2, waiting for transfers between devices, backward(): lax.all_to_all(pencils, axes, split_axis=0, concat_axis=1, tiled=True)  25.2 us
    ppermute x16, starting transfers between devices, partner(): return lax.ppermute(values, 'echo', [(e, e ^ offset) for e in range(4)])  20.4 us
    add x8, other arithmetic, on_device(): terms = (kept, arrived, partner(kept[1:] + arrived[1:], far))  12.5 us
  transfers between devices with their start and end apart: 25, of which 16 were waited for; matrix products, arithmetic and copies ran while one was open for 10% of the time, Pallas kernels for 19%

profile of v2, /device:TPU:0, one launch (start us, length us, event | category | flops | bytes accessed | tf_op | source)
XLA Modules:
  0.0 488.4 jit_solution(7516295775142729826)
XLA Ops:
  10.6 3.8 coil_sums.19
  22.8 3.8 coil_sums.21
  27.3 5.0 %coil_sums.23 = f32[2,17,2,32,256]{4,3,2,1,0:T(8,128)} custom-call(s32[1]{0:T(128)} %bitcast.place_ref, bf16[2,8,4,8,256,256]{5,4,3,2,1,0:T(8,128)(2,1)} %images_ref.31, bf16[2,4,8,256,256]{4,3,2,1,0:T(8,128)(2,1)S(1)} %copy-done), custom_call_target="tpu_custom_call" | custom-call | flops 8388608 | bytes 6946816 | tf_op jit(solution)/shard_map/coil_sums/pallas_call | solution.py:74
  32.3 5.0 %coil_sums.25 = f32[2,17,2,32,256]{4,3,2,1,0:T(8,128)} custom-call(s32[1]{0:T(128)} %bitcast.place_ref, bf16[2,8,4,8,256,256]{5,4,3,2,1,0:T(8,128)(2,1)} %images_ref.31, bf16[2,4,8,256,256]{4,3,2,1,0:T(8,128)(2,1)S(1)} %copy-done), custom_call_target="tpu_custom_call" | custom-call | flops 8388608 | bytes 6946816 | tf_op jit(solution)/shard_map/coil_sums/pallas_call | solution.py:74
  39.2 4.9 %coil_sums.27 = f32[2,17,2,32,256]{4,3,2,1,0:T(8,128)} custom-call(s32[1]{0:T(128)} %bitcast.place_ref, bf16[2,8,4,8,256,256]{5,4,3,2,1,0:T(8,128)(2,1)} %images_ref.31, bf16[2,4,8,256,256]{4,3,2,1,0:T(8,128)(2,1)S(1)} %copy-done), custom_call_target="tpu_custom_call" | custom-call | flops 8388608 | bytes 6946816 | tf_op jit(solution)/shard_map/coil_sums/pallas_call | solution.py:74
  44.1 22.6 %collective-permute-done.2.refs_1_ = f32[2,17,2,32,256]{4,3,2,1,0:T(8,128)S(1)} collective-permute-done((f32[2,17,2,32,256]{4,3,2,1,0:T(8,128)S(1)}, f32[2,17,2,32,256]{4,3,2,1,0:T(8,128)S(1)}, u32[]{:S(2)}, u32[]{:S(2)}) %collective-permute-start.2) | collective-permute-done | bytes 2228256 | tf_op jit(solution)/shard_map/ppermute | solution.py:219
  68.8 5.0 %coil_sums.29 = f32[2,17,2,32,256]{4,3,2,1,0:T(8,128)} custom-call(s32[1]{0:T(128)} %bitcast.place_ref, bf16[2,8,4,8,256,256]{5,4,3,2,1,0:T(8,128)(2,1)} %images_ref.31, bf16[2,4,8,256,256]{4,3,2,1,0:T(8,128)(2,1)S(1)} %copy-done), custom_call_target="tpu_custom_call" | custom-call | flops 8388608 | bytes 6946816 | tf_op jit(solution)/shard_map/coil_sums/pallas_call | solution.py:74
  73.7 4.9 %coil_sums.31 = f32[2,17,2,32,256]{4,3,2,1,0:T(8,128)} custom-call(s32[1]{0:T(128)} %bitcast.place_ref, bf16[2,8,4,8,256,256]{5,4,3,2,1,0:T(8,128)(2,1)} %images_ref.31, bf16[2,4,8,256,256]{4,3,2,1,0:T(8,128)(2,1)S(1)} %copy-done), custom_call_target="tpu_custom_call" | custom-call | flops 8388608 | bytes 6946816 | tf_op jit(solution)/shard_map/coil_sums/pallas_call | solution.py:74
  80.2 40.3 %collective-permute-done.4.refs_1_ = f32[2,17,2,32,256]{4,3,2,1,0:T(8,128)S(1)} collective-permute-done((f32[2,17,2,32,256]{4,3,2,1,0:T(8,128)S(1)}, f32[2,17,2,32,256]{4,3,2,1,0:T(8,128)S(1)}, u32[]{:S(2)}, u32[]{:S(2)}) %collective-permute-start.4) | collective-permute-done | bytes 2228256 | tf_op jit(solution)/shard_map/ppermute | solution.py:219
  120.5 4.7 coil_sums.18.refs_0_
  125.2 4.7 coil_sums.16.refs_0_
  129.8 4.7 coil_sums.20.refs_0_
  134.5 4.7 coil_sums.22.refs_0_
  139.2 4.7 coil_sums.24.refs_0_
  143.8 4.7 coil_sums.26.refs_0_
  148.5 4.7 coil_sums.28.refs_0_
  157.6 10.7 %collective-permute-done.8.refs_1_ = f32[2,17,2,32,256]{4,3,2,1,0:T(8,128)} collective-permute-done((f32[2,17,2,32,256]{4,3,2,1,0:T(8,128)}, f32[2,17,2,32,256]{4,3,2,1,0:T(8,128)}, u32[]{:S(2)}, u32[]{:S(2)}) %collective-permute-start.8) | collective-permute-done | bytes 2228256 | tf_op jit(solution)/shard_map/ppermute | solution.py:219
  176.8 39.3 %collective-permute-done.12.refs_1_ = f32[2,17,2,32,256]{4,3,2,1,0:T(8,128)} collective-permute-done((f32[2,17,2,32,256]{4,3,2,1,0:T(8,128)}, f32[2,17,2,32,256]{4,3,2,1,0:T(8,128)}, u32[]{:S(2)}, u32[]{:S(2)}) %collective-permute-start.12) | collective-permute-done | bytes 2228256 | tf_op jit(solution)/shard_map/ppermute | solution.py:219
  218.1 21.8 %collective-permute-done.3.refs_2_ = f32[1,17,2,32,256]{4,3,2,1,0:T(8,128)S(1)} collective-permute-done((f32[1,17,2,32,256]{4,3,2,1,0:T(8,128)S(1)}, f32[1,17,2,32,256]{4,3,2,1,0:T(8,128)S(1)}, u32[]{:S(2)}, u32[]{:S(2)}) %collective-permute-start.3) | collective-permute-done | bytes 1114144 | tf_op jit(solution)/shard_map/ppermute | solution.py:219
  251.4 6.4 %collective-permute-done.5.refs_2_ = f32[1,17,2,32,256]{4,3,2,1,0:T(8,128)} collective-permute-done((f32[1,17,2,32,256]{4,3,2,1,0:T(8,128)S(1)}, f32[1,17,2,32,256]{4,3,2,1,0:T(8,128)}, u32[]{:S(2)}, u32[]{:S(2)}) %collective-permute-start.5) | collective-permute-done | bytes 1114144 | tf_op jit(solution)/shard_map/ppermute | solution.py:219
  276.1 5.6 %collective-permute-done.9.refs_2_ = f32[1,17,2,32,256]{4,3,2,1,0:T(8,128)} collective-permute-done((f32[1,17,2,32,256]{4,3,2,1,0:T(8,128)S(1)}, f32[1,17,2,32,256]{4,3,2,1,0:T(8,128)}, u32[]{:S(2)}, u32[]{:S(2)}) %collective-permute-start.9) | collective-permute-done | bytes 1114144 | tf_op jit(solution)/shard_map/ppermute | solution.py:219
  291.1 13.6 %collective-permute-done.13.refs_2_ = f32[1,17,2,32,256]{4,3,2,1,0:T(8,128)} collective-permute-done((f32[1,17,2,32,256]{4,3,2,1,0:T(8,128)}, f32[1,17,2,32,256]{4,3,2,1,0:T(8,128)}, u32[]{:S(2)}, u32[]{:S(2)}) %collective-permute-start.13) | collective-permute-done | bytes 1114144 | tf_op jit(solution)/shard_map/ppermute | solution.py:219
  316.8 5.3 %all-to-all-start = ((f32[2,256,256]{2,0,1:T(2,128)}), f32[2,256,256]{2,0,1:T(2,128)S(1)}, u32[]{:S(2)}, u32[]{:S(2)}) async-start(f32[2,256,256]{2,0,1:T(2,128)} %copy.86), calls=%async_computation | async-start | bytes 1048576 | tf_op jit(solution)/shard_map/all_to_all | solution.py:263
  322.9 15.5 %all-to-all-done = f32[2,256,256]{2,0,1:T(2,128)S(1)} async-done(((f32[2,256,256]{2,0,1:T(2,128)}), f32[2,256,256]{2,0,1:T(2,128)S(1)}, u32[]{:S(2)}, u32[]{:S(2)}) %all-to-all-start) | async-done | bytes 524320 | tf_op jit(solution)/shard_map/all_to_all | solution.py:263
  346.1 14.5 %all-to-all-done.1 = f32[64,8,256]{2,1,0:T(8,128)S(1)} async-done(((f32[64,8,256]{2,1,0:T(8,128)}), f32[64,8,256]{2,1,0:T(8,128)S(1)}, u32[]{:S(2)}, u32[]{:S(2)}) %all-to-all-start.1) | async-done | bytes 524320 | tf_op jit(solution)/shard_map/all_to_all | solution.py:268
  368.8 10.7 %all-to-all-done.6 = f32[64,8,256]{2,1,0:T(8,128)S(1)} async-done(((f32[64,8,256]{2,1,0:T(8,128)}), f32[64,8,256]{2,1,0:T(8,128)S(1)}, u32[]{:S(2)}, u32[]{:S(2)}) %all-to-all-start.6) | async-done | bytes 524320 | tf_op jit(solution)/shard_map/all_to_all | solution.py:268
  389.8 4.2 all-to-all-start.3
  396.6 13.7 %all-to-all-done.3 = f32[2,256,256]{2,0,1:T(2,128)S(1)} async-done(((f32[2,256,256]{2,0,1:T(2,128)}), f32[2,256,256]{2,0,1:T(2,128)S(1)}, u32[]{:S(2)}, u32[]{:S(2)}) %all-to-all-start.3) | async-done | bytes 524320 | tf_op jit(solution)/shard_map/all_to_all | solution.py:263
  413.8 18.4 %all_to_all.118 = f32[64,8,256]{2,1,0:T(8,128)S(1)} all-to-all(f32[64,8,256]{2,1,0:T(8,128)S(1)} %copy.107), channel_id=1, replica_groups=mesh['echo'=4,'space'=8] {'space','echo'}, dimensions={0} | all-to-all | bytes 1048576 | tf_op jit(solution)/shard_map/all_to_all | solution.py:268
  436.2 18.4 %all_to_all.119 = f32[64,8,256]{2,1,0:T(8,128)S(1)} all-to-all(f32[64,8,256]{2,1,0:T(8,128)S(1)} %copy.98), channel_id=1, replica_groups=mesh['echo'=4,'space'=8] {'space','echo'}, dimensions={0} | all-to-all | bytes 1048576 | tf_op jit(solution)/shard_map/all_to_all | solution.py:268
  463.0 7.1 %all-to-all-done.5 = f32[32,1,128]{2,1,0:T(1,128)S(1)} async-done(((f32[32,1,128]{2,1,0:T(1,128)}), f32[32,1,128]{2,1,0:T(1,128)S(1)}, u32[]{:S(2)}, u32[]{:S(2)}) %all-to-all-start.5) | async-done | bytes 16416 | tf_op jit(solution)/shard_map/all_to_all | solution.py:276
  476.6 4.0 multiply_add_fusion
  (171 shorter events, 129.2 us)
Async XLA Ops:
  14.4 52.3 %collective-permute-start.2 = (f32[2,17,2,32,256]{4,3,2,1,0:T(8,128)S(1)}, f32[2,17,2,32,256]{4,3,2,1,0:T(8,128)S(1)}, u32[]{:S(2)}, u32[]{:S(2)}) collective-permute-start(f32[2,17,2,32,256]{4,3,2,1,0:T(8,128)S(1)} %coil_sums.19), channel_id=1, source_target_pairs={{0,16},{8,24},{16,0},{24,8},{1,17},{9,25},{17,1},{25,9},{2,18},{10... | collective-permute-start | bytes 6684680 | tf_op jit(solution)/shard_map/ppermute | solution.py:219
  21.3 57.4 %collective-permute-start = (f32[2,17,2,32,256]{4,3,2,1,0:T(8,128)S(1)}, f32[2,17,2,32,256]{4,3,2,1,0:T(8,128)S(1)}, u32[]{:S(2)}, u32[]{:S(2)}) collective-permute-start(f32[2,17,2,32,256]{4,3,2,1,0:T(8,128)S(1)} %coil_sums.17), channel_id=1, source_target_pairs={{0,8},{8,0},{16,24},{24,16},{1,9},{9,1},{17,25},{25,17},{2,10},{10... | collective-permute-start | bytes 6684680 | tf_op jit(solution)/shard_map/ppermute | solution.py:219
  26.7 93.8 %collective-permute-start.4 = (f32[2,17,2,32,256]{4,3,2,1,0:T(8,128)S(1)}, f32[2,17,2,32,256]{4,3,2,1,0:T(8,128)S(1)}, u32[]{:S(2)}, u32[]{:S(2)}) collective-permute-start(f32[2,17,2,32,256]{4,3,2,1,0:T(8,128)S(1)} %coil_sums.21), channel_id=1, source_target_pairs={{0,8},{8,0},{16,24},{24,16},{1,9},{9,1},{17,25},{25,17},{2,10},{10... | collective-permute-start | bytes 6684680 | tf_op jit(solution)/shard_map/ppermute | solution.py:219
  32.2 123.6 %collective-permute-start.6 = (f32[2,17,2,32,256]{4,3,2,1,0:T(8,128)}, f32[2,17,2,32,256]{4,3,2,1,0:T(8,128)}, u32[]{:S(2)}, u32[]{:S(2)}) collective-permute-start(f32[2,17,2,32,256]{4,3,2,1,0:T(8,128)} %coil_sums.23), channel_id=1, source_target_pairs={{0,16},{8,24},{16,0},{24,8},{1,17},{9,25},{17,1},{25,9},{2,18},{10... | collective-permute-start | bytes 6684680 | tf_op jit(solution)/shard_map/ppermute | solution.py:219
  37.2 131.1 %collective-permute-start.8 = (f32[2,17,2,32,256]{4,3,2,1,0:T(8,128)}, f32[2,17,2,32,256]{4,3,2,1,0:T(8,128)}, u32[]{:S(2)}, u32[]{:S(2)}) collective-permute-start(f32[2,17,2,32,256]{4,3,2,1,0:T(8,128)} %coil_sums.25), channel_id=1, source_target_pairs={{0,8},{8,0},{16,24},{24,16},{1,9},{9,1},{17,25},{25,17},{2,10},{10... | collective-permute-start | bytes 6684680 | tf_op jit(solution)/shard_map/ppermute | solution.py:219
  66.7 105.5 %collective-permute-start.10 = (f32[2,17,2,32,256]{4,3,2,1,0:T(8,128)}, f32[2,17,2,32,256]{4,3,2,1,0:T(8,128)}, u32[]{:S(2)}, u32[]{:S(2)}) collective-permute-start(f32[2,17,2,32,256]{4,3,2,1,0:T(8,128)} %coil_sums.27), channel_id=1, source_target_pairs={{0,16},{8,24},{16,0},{24,8},{1,17},{9,25},{17,1},{25,9},{2,18},{10... | collective-permute-start | bytes 6684680 | tf_op jit(solution)/shard_map/ppermute | solution.py:219
  78.7 41.8 %copy-start.12 = (f32[2,17,2,32,256]{4,3,2,1,0:T(8,128)}, f32[2,17,2,32,256]{4,3,2,1,0:T(8,128)S(1)}, u32[]{:S(2)}) copy-start(f32[2,17,2,32,256]{4,3,2,1,0:T(8,128)S(1)} %collective-permute-done.refs_1_) | copy-start | bytes 6684676
  78.7 137.4 %collective-permute-start.12 = (f32[2,17,2,32,256]{4,3,2,1,0:T(8,128)}, f32[2,17,2,32,256]{4,3,2,1,0:T(8,128)}, u32[]{:S(2)}, u32[]{:S(2)}) collective-permute-start(f32[2,17,2,32,256]{4,3,2,1,0:T(8,128)} %coil_sums.29), channel_id=1, source_target_pairs={{0,8},{8,0},{16,24},{24,16},{1,9},{9,1},{17,25},{25,17},{2,10},{10... | collective-permute-start | bytes 6684680 | tf_op jit(solution)/shard_map/ppermute | solution.py:219
  120.5 97.1 %collective-permute-start.14 = (f32[2,17,2,32,256]{4,3,2,1,0:T(8,128)}, f32[2,17,2,32,256]{4,3,2,1,0:T(8,128)}, u32[]{:S(2)}, u32[]{:S(2)}) collective-permute-start(f32[2,17,2,32,256]{4,3,2,1,0:T(8,128)} %coil_sums.31), channel_id=1, source_target_pairs={{0,16},{8,24},{16,0},{24,8},{1,17},{9,25},{17,1},{25,9},{2,18},{10... | collective-permute-start | bytes 6684680 | tf_op jit(solution)/shard_map/ppermute | solution.py:219
  125.1 28.1 %copy-start.8 = (f32[2,17,2,32,256]{4,3,2,1,0:T(8,128)}, f32[2,17,2,32,256]{4,3,2,1,0:T(8,128)S(1)}, u32[]{:S(2)}) copy-start(f32[2,17,2,32,256]{4,3,2,1,0:T(8,128)S(1)} %coil_sums.18.refs_0_) | copy-start | bytes 6684676
  129.8 23.7 %copy-start.7 = (f32[2,17,2,32,256]{4,3,2,1,0:T(8,128)}, f32[2,17,2,32,256]{4,3,2,1,0:T(8,128)S(1)}, u32[]{:S(2)}) copy-start(f32[2,17,2,32,256]{4,3,2,1,0:T(8,128)S(1)} %coil_sums.16.refs_0_) | copy-start | bytes 6684676
  139.2 29.2 %copy-start.4 = (f32[2,17,2,32,256]{4,3,2,1,0:T(8,128)}, f32[2,17,2,32,256]{4,3,2,1,0:T(8,128)S(1)}, u32[]{:S(2)}) copy-start(f32[2,17,2,32,256]{4,3,2,1,0:T(8,128)S(1)} %coil_sums.22.refs_0_) | copy-start | bytes 6684676
  143.8 26.9 %copy-start.3 = (f32[2,17,2,32,256]{4,3,2,1,0:T(8,128)}, f32[2,17,2,32,256]{4,3,2,1,0:T(8,128)S(1)}, u32[]{:S(2)}) copy-start(f32[2,17,2,32,256]{4,3,2,1,0:T(8,128)S(1)} %coil_sums.24.refs_0_) | copy-start | bytes 6684676
  148.5 25.8 %copy-start.2 = (f32[2,17,2,32,256]{4,3,2,1,0:T(8,128)}, f32[2,17,2,32,256]{4,3,2,1,0:T(8,128)S(1)}, u32[]{:S(2)}) copy-start(f32[2,17,2,32,256]{4,3,2,1,0:T(8,128)S(1)} %coil_sums.26.refs_0_) | copy-start | bytes 6684676
  153.3 88.1 %copy-start.1 = (f32[2,17,2,32,256]{4,3,2,1,0:T(8,128)}, f32[2,17,2,32,256]{4,3,2,1,0:T(8,128)S(1)}, u32[]{:S(2)}) copy-start(f32[2,17,2,32,256]{4,3,2,1,0:T(8,128)S(1)} %coil_sums.28.refs_0_) | copy-start | bytes 6684676
  155.9 83.9 %collective-permute-start.3 = (f32[1,17,2,32,256]{4,3,2,1,0:T(8,128)S(1)}, f32[1,17,2,32,256]{4,3,2,1,0:T(8,128)S(1)}, u32[]{:S(2)}, u32[]{:S(2)}) collective-permute-start(f32[1,17,2,32,256]{4,3,2,1,0:T(8,128)S(1)} %slice_add_fusion.6), channel_id=1, source_target_pairs={{0,8},{8,0},{16,24},{24,16},{1,9},{9,1},{17,25},{25,17},{2,10},{10... | collective-permute-start | bytes 3342344 | tf_op jit(solution)/shard_map/ppermute | solution.py:219
  168.3 75.5 %collective-permute-start.1 = (f32[1,17,2,32,256]{4,3,2,1,0:T(8,128)S(1)}, f32[1,17,2,32,256]{4,3,2,1,0:T(8,128)S(1)}, u32[]{:S(2)}, u32[]{:S(2)}) collective-permute-start(f32[1,17,2,32,256]{4,3,2,1,0:T(8,128)S(1)} %slice_add_fusion.7), channel_id=1, source_target_pairs={{0,16},{8,24},{16,0},{24,8},{1,17},{9,25},{17,1},{25,9},{2,18},{10... | collective-permute-start | bytes 3342344 | tf_op jit(solution)/shard_map/ppermute | solution.py:219
  172.2 85.6 %collective-permute-start.5 = (f32[1,17,2,32,256]{4,3,2,1,0:T(8,128)S(1)}, f32[1,17,2,32,256]{4,3,2,1,0:T(8,128)}, u32[]{:S(2)}, u32[]{:S(2)}) collective-permute-start(f32[1,17,2,32,256]{4,3,2,1,0:T(8,128)S(1)} %slice_add_fusion.5), channel_id=1, source_target_pairs={{0,16},{8,24},{16,0},{24,8},{1,17},{9,25},{17,1},{25,9},{2,18},{10... | collective-permute-start | bytes 3342344 | tf_op jit(solution)/shard_map/ppermute | solution.py:219
  216.1 56.6 %collective-permute-start.7 = (f32[1,17,2,32,256]{4,3,2,1,0:T(8,128)}, f32[1,17,2,32,256]{4,3,2,1,0:T(8,128)}, u32[]{:S(2)}, u32[]{:S(2)}) collective-permute-start(f32[1,17,2,32,256]{4,3,2,1,0:T(8,128)} %slice_add_fusion.4), channel_id=1, source_target_pairs={{0,8},{8,0},{16,24},{24,16},{1,9},{9,1},{17,25},{25,17},{2,10},{10... | collective-permute-start | bytes 3342344 | tf_op jit(solution)/shard_map/ppermute | solution.py:219
  217.6 64.1 %collective-permute-start.9 = (f32[1,17,2,32,256]{4,3,2,1,0:T(8,128)S(1)}, f32[1,17,2,32,256]{4,3,2,1,0:T(8,128)}, u32[]{:S(2)}, u32[]{:S(2)}) collective-permute-start(f32[1,17,2,32,256]{4,3,2,1,0:T(8,128)S(1)} %slice_add_fusion.3), channel_id=1, source_target_pairs={{0,16},{8,24},{16,0},{24,8},{1,17},{9,25},{17,1},{25,9},{2,18},{10... | collective-permute-start | bytes 3342344 | tf_op jit(solution)/shard_map/ppermute | solution.py:219
  239.8 47.9 %collective-permute-start.11 = (f32[1,17,2,32,256]{4,3,2,1,0:T(8,128)}, f32[1,17,2,32,256]{4,3,2,1,0:T(8,128)}, u32[]{:S(2)}, u32[]{:S(2)}) collective-permute-start(f32[1,17,2,32,256]{4,3,2,1,0:T(8,128)} %slice_add_fusion.2), channel_id=1, source_target_pairs={{0,8},{8,0},{16,24},{24,16},{1,9},{9,1},{17,25},{25,17},{2,10},{10... | collective-permute-start | bytes 3342344 | tf_op jit(solution)/shard_map/ppermute | solution.py:219
  243.8 60.9 %collective-permute-start.13 = (f32[1,17,2,32,256]{4,3,2,1,0:T(8,128)}, f32[1,17,2,32,256]{4,3,2,1,0:T(8,128)}, u32[]{:S(2)}, u32[]{:S(2)}) collective-permute-start(f32[1,17,2,32,256]{4,3,2,1,0:T(8,128)} %slice_add_fusion.1), channel_id=1, source_target_pairs={{0,16},{8,24},{16,0},{24,8},{1,17},{9,25},{17,1},{25,9},{2,18},{10... | collective-permute-start | bytes 3342344 | tf_op jit(solution)/shard_map/ppermute | solution.py:219
  257.8 52.3 %collective-permute-start.15 = (f32[1,17,2,32,256]{4,3,2,1,0:T(8,128)}, f32[1,17,2,32,256]{4,3,2,1,0:T(8,128)}, u32[]{:S(2)}, u32[]{:S(2)}) collective-permute-start(f32[1,17,2,32,256]{4,3,2,1,0:T(8,128)} %slice_add_fusion), channel_id=1, source_target_pairs={{0,8},{8,0},{16,24},{24,16},{1,9},{9,1},{17,25},{25,17},{2,10},{10... | collective-permute-start | bytes 3342344 | tf_op jit(solution)/shard_map/ppermute | solution.py:219
  316.8 21.5 %all-to-all-start = ((f32[2,256,256]{2,0,1:T(2,128)}), f32[2,256,256]{2,0,1:T(2,128)S(1)}, u32[]{:S(2)}, u32[]{:S(2)}) async-start(f32[2,256,256]{2,0,1:T(2,128)} %copy.86), calls=%async_computation | async-start | bytes 1048576 | tf_op jit(solution)/shard_map/all_to_all | solution.py:263
  322.1 140.9 %all-gather.4.cloned.1.call-start = ((), (), s32[]{:S(2)}) async-start(), calls=%async_computation.8 | async-start | bytes 2621440 | tf_op jit(solution)/shard_map/all_gather | solution.py:241
  341.8 18.9 %all-to-all-start.1 = ((f32[64,8,256]{2,1,0:T(8,128)}), f32[64,8,256]{2,1,0:T(8,128)S(1)}, u32[]{:S(2)}, u32[]{:S(2)}) async-start(f32[64,8,256]{2,1,0:T(8,128)} %copy.89), calls=%async_computation.1 | async-start | bytes 1048576 | tf_op jit(solution)/shard_map/all_to_all | solution.py:268
  360.6 18.9 %all-to-all-start.6 = ((f32[64,8,256]{2,1,0:T(8,128)}), f32[64,8,256]{2,1,0:T(8,128)S(1)}, u32[]{:S(2)}, u32[]{:S(2)}) async-start(f32[64,8,256]{2,1,0:T(8,128)} %copy.103), calls=%async_computation.6 | async-start | bytes 1048576 | tf_op jit(solution)/shard_map/all_to_all | solution.py:268
  380.1 9.7 %all-to-all-start.2 = ((f32[32,1,128]{2,1,0:T(1,128)}), f32[32,1,128]{2,1,0:T(1,128)S(1)}, u32[]{:S(2)}, u32[]{:S(2)}) async-start(f32[32,1,128]{2,1,0:T(1,128)} %broadcast_in_dim.18), calls=%async_computation.2 | async-start | bytes 32768 | tf_op jit(solution)/shard_map/all_to_all | solution.py:276
  382.7 93.9 %all-gather.6.cloned.1.call-start = ((), (), s32[]{:S(2)}) async-start(), calls=%async_computation.9 | async-start | bytes 2621440 | tf_op jit(solution)/shard_map/all_gather | solution.py:241
  389.8 20.4 %all-to-all-start.3 = ((f32[2,256,256]{2,0,1:T(2,128)}), f32[2,256,256]{2,0,1:T(2,128)S(1)}, u32[]{:S(2)}, u32[]{:S(2)}) async-start(f32[2,256,256]{2,0,1:T(2,128)} %copy.95), calls=%async_computation.3 | async-start | bytes 1048576 | tf_op jit(solution)/shard_map/all_to_all | solution.py:263
  394.0 82.6 %all-gather.8.cloned.1.call-start = ((), (), s32[]{:S(2)}) async-start(), calls=%async_computation.10 | async-start | bytes 2621440 | tf_op jit(solution)/shard_map/all_gather | solution.py:241
  460.5 9.7 %all-to-all-start.5 = ((f32[32,1,128]{2,1,0:T(1,128)}), f32[32,1,128]{2,1,0:T(1,128)S(1)}, u32[]{:S(2)}, u32[]{:S(2)}) async-start(f32[32,1,128]{2,1,0:T(1,128)} %broadcast_in_dim.30), calls=%async_computation.5 | async-start | bytes 32768 | tf_op jit(solution)/shard_map/all_to_all | solution.py:276
  (24 other events, 166.8 us)
Sparse Core Ops, SparseCore 0:
  325.4 39.8 all-gather.3
  385.7 47.2 all-gather.5
  435.4 37.2 all-gather.7
